TPU v7x, 32 devices: a whole 2x2x4 slice. The times are simulated.
32 devices in a mesh: role: 2 (over y), tile: 16 (over z, x, core).
Axes of the slice: x: 2, y: 2, z: 4, core: 2. Of those that a mesh axis runs over, the one named last changes fastest.
Arguments:
- fields_pair: float32 [2, 512, 16384], P('role', None, 'tile'), may hold values from 0 to 1
- velocity: float32 [16384], P('tile'), may hold values from -0.5 to 0.5
- growth: float32 [16384], P('tile'), may hold values from 0.05 to 0.5
- features: bfloat16 [512, 1024], replicated, may hold values from -6 to 6
- assignment: int32 [512], replicated, may hold values from 0 to 511, each once
- out_pair: float32 [2, 1024, 16384], P('role', None, 'tile'), may hold values from -0.1875 to 0.1875
- hidden_pair: float32 [2, 5, 1024, 1024], P('role', None, 'tile'), may hold values from -0.1875 to 0.1875
Outputs:
- fields_next: float32 [2, 512, 16384], P('role', None, 'tile')
- out_next: float32 [2, 1024, 16384], P('role', None, 'tile')
- hidden_next: float32 [2, 5, 1024, 1024], P('role', None, 'tile')
Inputs may be any that keep to these rules, and one draw needn't show every extreme that they name: `assignment`: a permutation of the 512 members.
All inputs are finite; a program needn't handle non-finite values.
Results may differ from a plain program's by a relative error of at most 0.0022.
The roundings to bfloat16 on the way count: a program that leaves them out, or rounds other values in their place, can miss the bound.
Values may be sent and summed in bfloat16 or wider, within the bound.
A program may use at most 192 MiB of HBM per device.

v0:
```python
import jax
import jax.numpy as jnp
from jax import lax
from jax.sharding import PartitionSpec as P

momentum_decay = 0.9
step_size = 0.1


def extended(value, axis, dim, width):
    count, length = (lax.axis_size(axis), value.shape[dim])
    up = [(i, (i + 1) % count) for i in range(count)]
    down = [(j, i) for i, j in up]
    last = lax.slice_in_dim(value, length - width, length, axis=dim)
    leading = lax.slice_in_dim(value, 0, width, axis=dim)
    before = lax.ppermute(last, axis, up)
    after = lax.ppermute(leading, axis, down)
    return jnp.concatenate([before, value, after], axis=dim)


def silu_slope(values):
    logistic = jax.nn.sigmoid(values)
    return logistic * (1.0 + values * (1.0 - logistic))


def advance(padded, growth):
    states = padded[:-1]
    velocity_row = padded[-1]
    outflow = (
        jnp.maximum(velocity_row[:-1], 0.0) * states[:, :-1]
        + jnp.minimum(velocity_row[:-1], 0.0) * states[:, 1:]
    )
    carried = states[:, 1:-1] - outflow[:, 1:] + outflow[:, :-1]
    return carried + growth * carried * (1.0 - carried)


def to_trainer(value):
    return lax.ppermute(value.astype(jnp.bfloat16), "role", [(0, 1)])


def to_solver(value):
    return lax.ppermute(value.astype(jnp.bfloat16), "role", [(1, 0)])


def plain_training(features, hidden_narrow, out_narrow, own_fields, own_out, own_hidden):
    layer_count, unit_rows = own_hidden.shape[:2]
    batch = own_fields.shape[0]
    first_unit = lax.axis_index("tile") * unit_rows
    momentum_out = to_trainer(own_out)
    momentum_hidden = to_trainer(own_hidden)
    full_hidden = [
        lax.all_gather(hidden_narrow[i], "tile", axis=0, tiled=True) for i in range(layer_count)
    ]
    inputs, summed_list = ([], [])
    activation = features
    for i in range(layer_count):
        inputs.append(activation)
        summed = jnp.dot(activation, full_hidden[i], preferred_element_type=jnp.float32)
        summed_list.append(summed)
        activation = jax.nn.silu(summed).astype(jnp.bfloat16)
    predicted = jnp.dot(activation, out_narrow, preferred_element_type=jnp.float32)
    residual = ((predicted - own_fields) / batch).astype(jnp.bfloat16)
    partial_grad = lax.dot_general(
        residual, out_narrow, (((1,), (1,)), ((), ())), preferred_element_type=jnp.float32
    )
    upstream = lax.psum(partial_grad, "tile")
    grad_out = jnp.dot(activation.T, residual, preferred_element_type=jnp.float32)
    sent_out = to_solver(grad_out)
    gradients, sent = ([], [])
    for i in reversed(range(layer_count)):
        slope = (upstream * silu_slope(summed_list[i])).astype(jnp.bfloat16)
        own_inputs = lax.dynamic_slice_in_dim(inputs[i], first_unit, unit_rows, 1)
        gradient = jnp.dot(own_inputs.T, slope, preferred_element_type=jnp.float32)
        gradients.append(gradient)
        sent.append(to_solver(gradient))
        if i > 0:
            upstream = lax.dot_general(
                slope, full_hidden[i], (((1,), (1,)), ((), ())), preferred_element_type=jnp.float32
            )
    solver_side = lax.axis_index("role") == 0
    other_out = jnp.where(solver_side, sent_out, momentum_out)
    other_hidden = jnp.where(solver_side, jnp.stack(sent[::-1]), momentum_hidden)
    return (grad_out, jnp.stack(gradients[::-1]), other_out, other_hidden)


def body(fields_pair, velocity, growth, features, assignment, out_pair, hidden_pair):
    solver_side = lax.axis_index("role") == 0
    own_fields = fields_pair[0]
    own_out = out_pair[0]
    own_hidden = hidden_pair[0]
    stacked = jnp.concatenate([own_fields, velocity[None, :]], axis=0)
    advanced = advance(extended(stacked, "tile", 1, 1), growth)
    fresh_fields = to_trainer(advanced)
    grad_out, grad_hidden, other_out, other_hidden = plain_training(
        features,
        own_hidden.astype(jnp.bfloat16),
        own_out.astype(jnp.bfloat16),
        own_fields,
        own_out,
        own_hidden,
    )
    grad_out, grad_hidden, other_out, other_hidden = (
        v.astype(jnp.float32) for v in (grad_out, grad_hidden, other_out, other_hidden)
    )
    out_next = jnp.where(
        solver_side,
        momentum_decay * own_out + other_out,
        own_out - step_size * (momentum_decay * other_out + grad_out),
    )
    hidden_next = jnp.where(
        solver_side,
        momentum_decay * own_hidden + other_hidden,
        own_hidden - step_size * (momentum_decay * other_hidden + grad_hidden),
    )
    next_batch = jnp.take(fresh_fields, assignment, axis=0).astype(jnp.float32)
    fields_next = jnp.where(solver_side, advanced, next_batch)
    return (fields_next[None], out_next[None], hidden_next[None])


def solution(mesh):
    return jax.shard_map(
        body,
        mesh=mesh,
        in_specs=(
            P("role", None, "tile"),
            P("tile"),
            P("tile"),
            P(),
            P(),
            P("role", None, "tile"),
            P("role", None, "tile", None),
        ),
        out_specs=(P("role", None, "tile"), P("role", None, "tile"), P("role", None, "tile", None)),
        check_vma=False,
    )
```

profile of v0, /device:TPU:0, one launch (start us, length us, event | category | flops | bytes accessed | tf_op | source)
XLA Modules:
  0.0 390.6 jit_solution(13564146009136946338)
XLA Ops:
  7.2 0.0 all-gather.11.cloned.1.call-start
  7.2 1.5 bitcast_convert_fusion.1
  8.7 0.8 copy-done.6
  9.5 0.8 fusion.60
  10.4 0.0 all-gather.13.cloned.1.call-start
  10.5 0.7 all-gather.13.cloned.1.call-update
  11.2 0.0 all-gather.15.cloned.1.call-start
  11.2 0.7 all-gather.15.cloned.1.call-update
  11.9 0.0 all-gather.17.cloned.1.call-start
  11.9 0.5 all-gather.17.cloned.1.call-update
  12.5 0.0 all-gather.19.cloned.1.call-start
  12.5 0.5 all-gather.19.cloned.1.call-update
  13.1 5.9 %collective-permute-start.10 = (bf16[5,64,1024]{2,1,0:T(8,128)(2,1)}, bf16[5,64,1024]{2,1,0:T(8,128)(2,1)}, u32[]{:S(2)}, u32[]{:S(2)}) collective-permute-start(bf16[5,64,1024]{2,1,0:T(8,128)(2,1)} %copy-done.6), channel_id=1, source_target_pairs={{0,16},{1,17},{2,18},{3,19},{4,20},{5,21},{6,22},{7,23},{8,24},{9,... | collective-permute-start | bytes 1966088 | tf_op jit(solution)/shard_map/ppermute | solution.py:38
  19.0 4.0 %bitcast_convert_fusion = bf16[1024,1024]{1,0:T(8,128)(2,1)} fusion(f32[1,1024,1024]{2,1,0:T(8,128)} %param.12), kind=kLoop, calls=%fused_computation.8 | loop fusion | flops 1048576 | bytes 6291456 | tf_op jit(solution)/shard_map/convert_element_type | solution.py:97
  23.0 2.8 collective-permute-start.4
  25.8 0.1 pad_maximum_fusion.5
  25.9 0.1 collective-permute-start
  26.0 4.4 %collective-permute-start.1 = (f32[513,1]{1,0:T(8,128)S(1)}, f32[513,1]{1,0:T(8,128)S(1)}, u32[]{:S(2)}, u32[]{:S(2)}) collective-permute-start(f32[513,1]{1,0:T(8,128)S(1)} %get-tuple-element.8), channel_id=1, source_target_pairs={{1,0},{2,1},{3,2},{4,3},{5,4},{6,5},{7,6},{8,7},{9,8},{10,9},{11,1... | collective-permute-start | bytes 6164 | tf_op jit(solution)/shard_map/ppermute | solution.py:17
  30.4 5.4 %collective-permute-done = f32[513,1]{1,0:T(8,128)S(1)} collective-permute-done((f32[513,1]{1,0:T(8,128)S(1)}, f32[513,1]{1,0:T(8,128)S(1)}, u32[]{:S(2)}, u32[]{:S(2)}) %collective-permute-start) | collective-permute-done | bytes 2084 | tf_op jit(solution)/shard_map/ppermute | solution.py:16
  35.8 0.1 maximum_reduce_fusion
  36.0 0.7 fusion.6
  36.7 2.4 fusion.59
  39.1 1.5 collective-permute-start.2
  40.6 15.2 %all-gather.11.cloned.1.call-done = bf16[1,1024,1024]{2,1,0:T(8,128)(2,1)} async-done(((bf16[1,64,1024]{2,1,0:T(8,128)(2,1)}), bf16[1,1024,1024]{2,1,0:T(8,128)(2,1)}) %all-gather.11.cloned.1.call-update) | async-done | bytes 2097168 | tf_op jit(solution)/shard_map/all_gather | solution.py:52
  55.8 4.6 %multiply_convert_fusion.10 = (bf16[512,1024]{1,0:T(8,128)(2,1)}, f32[512,1024]{1,0:T(8,128)}) fusion(bf16[512,1024]{1,0:T(8,128)(2,1)S(1)} %copy-done, bf16[1,1024,1024]{2,1,0:T(8,128)(2,1)} %all-gather.11.cloned.1.call-done), kind=kOutput, calls=%fused_computation.51 | convolution fusion | flops 1076363264 | bytes 6291456 | tf_op jit(solution)/shard_map/dot_general | solution.py:58
  60.5 37.8 %all-gather.13.cloned.1.call-done = bf16[1,1024,1024]{2,1,0:T(8,128)(2,1)} async-done(((bf16[1,64,1024]{2,1,0:T(8,128)(2,1)}), bf16[1,1024,1024]{2,1,0:T(8,128)(2,1)}) %all-gather.13.cloned.1.call-update) | async-done | bytes 2097168 | tf_op jit(solution)/shard_map/all_gather | solution.py:52
  98.2 4.7 %multiply_convert_fusion.9 = (bf16[512,1024]{1,0:T(8,128)(2,1)S(1)}, f32[512,1024]{1,0:T(8,128)}) fusion(bf16[512,1024]{1,0:T(8,128)(2,1)} %get-tuple-element.14, bf16[1,1024,1024]{2,1,0:T(8,128)(2,1)} %all-gather.13.cloned.1.call-done), kind=kOutput, calls=%fused_computation.49 | convolution fusion | flops 1076363264 | bytes 6291456 | tf_op jit(solution)/shard_map/dot_general | solution.py:58
  102.9 37.7 %all-gather.15.cloned.1.call-done = bf16[1,1024,1024]{2,1,0:T(8,128)(2,1)} async-done(((bf16[1,64,1024]{2,1,0:T(8,128)(2,1)}), bf16[1,1024,1024]{2,1,0:T(8,128)(2,1)}) %all-gather.15.cloned.1.call-update) | async-done | bytes 2097168 | tf_op jit(solution)/shard_map/all_gather | solution.py:52
  140.6 4.7 %multiply_convert_fusion.8 = (bf16[512,1024]{1,0:T(8,128)(2,1)}, f32[512,1024]{1,0:T(8,128)}) fusion(bf16[512,1024]{1,0:T(8,128)(2,1)S(1)} %get-tuple-element.16, bf16[1,1024,1024]{2,1,0:T(8,128)(2,1)} %all-gather.15.cloned.1.call-done), kind=kOutput, calls=%fused_computation.47 | convolution fusion | flops 1076363264 | bytes 6291456 | tf_op jit(solution)/shard_map/dot_general | solution.py:58
  145.3 37.5 %all-gather.17.cloned.1.call-done = bf16[1,1024,1024]{2,1,0:T(8,128)(2,1)} async-done(((bf16[1,64,1024]{2,1,0:T(8,128)(2,1)}), bf16[1,1024,1024]{2,1,0:T(8,128)(2,1)}) %all-gather.17.cloned.1.call-update) | async-done | bytes 2097168 | tf_op jit(solution)/shard_map/all_gather | solution.py:52
  182.8 4.7 %multiply_convert_fusion.7 = (bf16[512,1024]{1,0:T(8,128)(2,1)S(1)}, f32[512,1024]{1,0:T(8,128)}) fusion(bf16[512,1024]{1,0:T(8,128)(2,1)} %get-tuple-element.18, bf16[1,1024,1024]{2,1,0:T(8,128)(2,1)} %all-gather.17.cloned.1.call-done), kind=kOutput, calls=%fused_computation.45 | convolution fusion | flops 1076363264 | bytes 6291456 | tf_op jit(solution)/shard_map/dot_general | solution.py:58
  187.6 38.1 %all-gather.19.cloned.1.call-done = bf16[1,1024,1024]{2,1,0:T(8,128)(2,1)} async-done(((bf16[1,64,1024]{2,1,0:T(8,128)(2,1)}), bf16[1,1024,1024]{2,1,0:T(8,128)(2,1)}) %all-gather.19.cloned.1.call-update) | async-done | bytes 2097168 | tf_op jit(solution)/shard_map/all_gather | solution.py:52
  225.6 3.0 fusion.10
  228.7 3.7 multiply_convert_fusion.5
  232.3 1.0 copy-done.19
  233.3 4.2 %fusion.64 = f32[512,1024]{1,0:T(8,128)} fusion(bf16[512,1024]{1,0:T(8,128)(2,1)S(1)} %multiply_convert_fusion.5, bf16[1024,1024]{1,0:T(8,128)(2,1)} %bitcast_convert_fusion), kind=kOutput, calls=%fused_computation.103 | convolution fusion | flops 1073741824 | bytes 5242880 | tf_op jit(solution)/shard_map/dot_general | solution.py:63
  237.6 2.1 gather_fusion
  239.6 3.4 select_bitcast_fusion
  243.0 4.1 %fusion.61 = (bf16[1024,1024]{1,0:T(8,128)(2,1)}, f32[1024,1024]{1,0:T(8,128)}) fusion(bf16[512,1024]{1,0:T(8,128)(2,1)S(1)} %copy-done.20, f32[512,1024]{1,0:T(8,128)S(1)} %copy-done.8), kind=kOutput, calls=%fused_computation.102 | convolution fusion | flops 1077411840 | bytes 9437184 | tf_op jit(solution)/shard_map/dot_general | solution.py:67
  247.1 1.5 collective-permute-start.3
  248.6 86.0 %all-reduce.2.cloned.1.call-done = f32[512,1024]{1,0:T(8,128)} async-done(((f32[512,1024]{1,0:T(8,128)}), f32[512,1024]{1,0:T(8,128)}) %all-reduce.2.cloned.1.call-update) | async-done | bytes 2097168 | tf_op jit(solution)/shard_map/psum | solution.py:66
  334.6 3.0 multiply_convert_fusion.4
  337.5 4.0 %multiply_convert_fusion.3 = bf16[512,1024]{1,0:T(8,128)(2,1)S(1)} fusion(f32[512,1024]{1,0:T(8,128)} %get-tuple-element.21, bf16[512,1024]{1,0:T(8,128)(2,1)S(1)} %multiply_convert_fusion.4, bf16[1,1024,1024]{2,1,0:T(8,128)(2,1)} %all-gather.19.cloned.1.call-done), kind=kOutput, calls=%fused_computation.40 | convolution fusion | flops 1078460416 | bytes 6291456 | tf_op jit(solution)/shard_map/dot_general | solution.py:77
  341.6 1.6 multiply_convert_fusion.2
  343.2 0.3 copy-done.17
  343.5 0.6 copy-done.21
  344.1 2.6 multiply_convert_fusion.1
  346.7 4.3 %bitcast_dynamic-update-slice_fusion.4 = (f32[5,64,1024]{2,1,0:T(8,128)S(1)}, bf16[64,1024]{1,0:T(8,128)(2,1)S(1)}) fusion(f32[512,1024]{1,0:T(8,128)} %get-tuple-element.15, bf16[512,1024]{1,0:T(8,128)(2,1)} %multiply_convert_fusion.1, bf16[1,1024,1024]{2,1,0:T(8,128)(2,1)} %all-gather.13.cloned.1.call-done, bf16[512,1024]{1,0:T(8,128)(2,1)S(1)} %copy-done, ...), kind=kOutput, calls=%fused_computation.72 | convolution fusion | flops 1145634816 | bytes 5767172 | tf_op jit(solution)/shard_map/dot_general | solution.py:73
  351.1 1.8 bitcast_dynamic-update-slice_fusion.3
  352.9 1.3 collective-permute-start.6
  354.2 1.3 collective-permute-start.5
  355.5 1.7 bitcast_dynamic-update-slice_fusion.2
  357.2 1.5 bitcast_dynamic-update-slice_fusion.1
  358.7 1.5 bitcast_dynamic-update-slice_fusion
  360.2 1.8 collective-permute-done.5
  362.0 1.3 collective-permute-start.7
  363.3 1.3 collective-permute-start.8
  364.6 4.2 %collective-permute-done.7 = bf16[64,1024]{1,0:T(8,128)(2,1)S(1)} collective-permute-done((bf16[64,1024]{1,0:T(8,128)(2,1)S(1)}, bf16[64,1024]{1,0:T(8,128)(2,1)S(1)}, u32[]{:S(2)}, u32[]{:S(2)}) %collective-permute-start.7) | collective-permute-done | bytes 131104 | tf_op jit(solution)/shard_map/ppermute | solution.py:42
  368.8 1.3 collective-permute-start.9
  370.1 0.1 collective-permute-done.8
  370.2 5.4 %collective-permute-done.9 = bf16[64,1024]{1,0:T(8,128)(2,1)S(1)} collective-permute-done((bf16[64,1024]{1,0:T(8,128)(2,1)S(1)}, bf16[64,1024]{1,0:T(8,128)(2,1)S(1)}, u32[]{:S(2)}, u32[]{:S(2)}) %collective-permute-start.9) | collective-permute-done | bytes 131104 | tf_op jit(solution)/shard_map/ppermute | solution.py:42
  375.7 1.6 fusion.35
  377.3 1.1 copy-done.3
  378.4 5.3 %fusion.1 = f32[1,1024,1024]{2,1,0:T(8,128)} fusion(f32[1024,1024]{1,0:T(8,128)S(1)} %copy-done.5, f32[1,1024,1024]{2,1,0:T(8,128)S(1)} %copy-done.3, bf16[1024,1024]{1,0:T(8,128)(2,1)} %collective-permute-done.3, bf16[1024,1024]{1,0:T(8,128)(2,1)} %collective-permute-done.4, pred[]{:T(512)S(6)} %eq.4), kind=kLoop, calls=%fused_computation.4 | loop fusion | flops 9437184 | bytes 16777216 | tf_op jit(solution)/shard_map/broadcast_in_dim | solution.py:117
  (58 shorter events, 0.3 us)
Async XLA Ops:
  7.2 48.7 %copy-start = (bf16[512,1024]{1,0:T(8,128)(2,1)S(1)}, bf16[512,1024]{1,0:T(8,128)(2,1)}, u32[]{:S(2)}) copy-start(bf16[512,1024]{1,0:T(8,128)(2,1)} %param.10) | copy-start | bytes 3145732
  7.2 48.7 %all-gather.11.cloned.1.call-start = ((), (), s32[]{:S(2)}) async-start(), calls=%async_computation.1 | async-start | bytes 2228224 | tf_op jit(solution)/shard_map/all_gather | solution.py:52
  8.7 0.8 copy-start.6
  10.4 87.8 %all-gather.13.cloned.1.call-start = ((), (), s32[]{:S(2)}) async-start(), calls=%async_computation.2 | async-start | bytes 2228224 | tf_op jit(solution)/shard_map/all_gather | solution.py:52
  11.2 129.5 %all-gather.15.cloned.1.call-start = ((), (), s32[]{:S(2)}) async-start(), calls=%async_computation.3 | async-start | bytes 2228224 | tf_op jit(solution)/shard_map/all_gather | solution.py:52
  11.9 170.9 %all-gather.17.cloned.1.call-start = ((), (), s32[]{:S(2)}) async-start(), calls=%async_computation.4 | async-start | bytes 2228224 | tf_op jit(solution)/shard_map/all_gather | solution.py:52
  12.5 213.2 %all-gather.19.cloned.1.call-start = ((), (), s32[]{:S(2)}) async-start(), calls=%async_computation.5 | async-start | bytes 2228224 | tf_op jit(solution)/shard_map/all_gather | solution.py:52
  13.1 12.7 %copy-start.1 = (f32[1,512,1024]{2,1,0:T(8,128)S(1)}, f32[1,512,1024]{2,1,0:T(8,128)}, u32[]{:S(2)}) copy-start(f32[1,512,1024]{2,1,0:T(8,128)} %param.7) | copy-start | bytes 6291460
  13.1 12.7 %copy-start.12 = (f32[1024]{0:T(1024)S(1)}, f32[1024]{0:T(1024)}, u32[]{:S(2)}) copy-start(f32[1024]{0:T(1024)} %param.8) | copy-start | bytes 12292
  13.1 321.5 %all-reduce.2.cloned.1.call-start = ((), (), s32[]{:S(2)}) async-start(), calls=%async_computation | async-start | bytes 4194304 | tf_op jit(solution)/shard_map/psum | solution.py:66
  13.1 362.6 %collective-permute-start.10 = (bf16[5,64,1024]{2,1,0:T(8,128)(2,1)}, bf16[5,64,1024]{2,1,0:T(8,128)(2,1)}, u32[]{:S(2)}, u32[]{:S(2)}) collective-permute-start(bf16[5,64,1024]{2,1,0:T(8,128)(2,1)} %copy-done.6), channel_id=1, source_target_pairs={{0,16},{1,17},{2,18},{3,19},{4,20},{5,21},{6,22},{7,23},{8,24},{9,... | collective-permute-start | bytes 1966088 | tf_op jit(solution)/shard_map/ppermute | solution.py:38
  23.0 7.4 %copy-start.15 = (s32[512]{0:T(512)S(1)}, s32[512]{0:T(512)}, u32[]{:S(2)}) copy-start(s32[512]{0:T(512)} %param.11) | copy-start | bytes 6148
  23.0 354.3 %collective-permute-start.4 = (bf16[1024,1024]{1,0:T(8,128)(2,1)}, bf16[1024,1024]{1,0:T(8,128)(2,1)}, u32[]{:S(2)}, u32[]{:S(2)}) collective-permute-start(bf16[1024,1024]{1,0:T(8,128)(2,1)} %bitcast_convert_fusion), channel_id=1, source_target_pairs={{0,16},{1,17},{2,18},{3,19},{4,20},{5,21},{6,22},{7,23},{8,24},{9,... | collective-permute-start | bytes 6291464 | tf_op jit(solution)/shard_map/ppermute | solution.py:38
  25.9 9.9 %collective-permute-start = (f32[513,1]{1,0:T(8,128)S(1)}, f32[513,1]{1,0:T(8,128)S(1)}, u32[]{:S(2)}, u32[]{:S(2)}) collective-permute-start(f32[513,1]{1,0:T(8,128)S(1)} %get-tuple-element.7), channel_id=1, source_target_pairs={{0,1},{1,2},{2,3},{3,4},{4,5},{5,6},{6,7},{7,8},{8,9},{9,10},{10,1... | collective-permute-start | bytes 6164 | tf_op jit(solution)/shard_map/ppermute | solution.py:16
  26.0 10.0 %collective-permute-start.1 = (f32[513,1]{1,0:T(8,128)S(1)}, f32[513,1]{1,0:T(8,128)S(1)}, u32[]{:S(2)}, u32[]{:S(2)}) collective-permute-start(f32[513,1]{1,0:T(8,128)S(1)} %get-tuple-element.8), channel_id=1, source_target_pairs={{1,0},{2,1},{3,2},{4,3},{5,4},{6,5},{7,6},{8,7},{9,8},{10,9},{11,1... | collective-permute-start | bytes 6164 | tf_op jit(solution)/shard_map/ppermute | solution.py:17
  35.9 0.7 copy-start.16
  39.1 198.5 %collective-permute-start.2 = (bf16[512,1024]{1,0:T(8,128)(2,1)}, bf16[512,1024]{1,0:T(8,128)(2,1)S(1)}, u32[]{:S(2)}, u32[]{:S(2)}) collective-permute-start(bf16[512,1024]{1,0:T(8,128)(2,1)} %get-tuple-element.5), channel_id=1, source_target_pairs={{0,16},{1,17},{2,18},{3,19},{4,20},{5,21},{6,22},{7,23},{8,24},{9,... | collective-permute-start | bytes 3145736 | tf_op jit(solution)/shard_map/ppermute | solution.py:38
  102.9 42.4 %copy-start.13 = (bf16[512,1024]{1,0:T(8,128)(2,1)}, bf16[512,1024]{1,0:T(8,128)(2,1)S(1)}, u32[]{:S(2)}) copy-start(bf16[512,1024]{1,0:T(8,128)(2,1)S(1)} %get-tuple-element.16) | copy-start | bytes 3145732
  187.5 41.1 %copy-start.14 = (bf16[512,1024]{1,0:T(8,128)(2,1)}, bf16[512,1024]{1,0:T(8,128)(2,1)S(1)}, u32[]{:S(2)}) copy-start(bf16[512,1024]{1,0:T(8,128)(2,1)S(1)} %get-tuple-element.20) | copy-start | bytes 3145732
  225.6 3.0 copy-start.2
  228.6 3.7 copy-start.7
  232.3 1.0 copy-start.19
  239.6 3.4 copy-start.8
  239.6 3.4 copy-start.20
  247.1 130.3 %collective-permute-start.3 = (bf16[1024,1024]{1,0:T(8,128)(2,1)}, bf16[1024,1024]{1,0:T(8,128)(2,1)}, u32[]{:S(2)}, u32[]{:S(2)}) collective-permute-start(bf16[1024,1024]{1,0:T(8,128)(2,1)} %get-tuple-element.22), channel_id=1, source_target_pairs={{16,0},{17,1},{18,2},{19,3},{20,4},{21,5},{22,6},{23,7},{24,8},{25... | collective-permute-start | bytes 6291464 | tf_op jit(solution)/shard_map/ppermute | solution.py:42
  337.5 4.0 %copy-start.18 = (bf16[1,1024,1024]{2,1,0:T(8,128)(2,1)S(1)}, bf16[1,1024,1024]{2,1,0:T(8,128)(2,1)}, u32[]{:S(2)}) copy-start(bf16[1,1024,1024]{2,1,0:T(8,128)(2,1)} %all-gather.17.cloned.1.call-done) | copy-start | bytes 6291460
  337.5 4.0 %copy-start.22 = (f32[512,1024]{1,0:T(8,128)S(1)}, f32[512,1024]{1,0:T(8,128)}, u32[]{:S(2)}) copy-start(f32[512,1024]{1,0:T(8,128)} %get-tuple-element.19) | copy-start | bytes 6291460
  341.5 1.7 copy-start.9
  341.5 2.0 copy-start.17
  341.5 2.6 copy-start.21
  343.2 3.5 copy-start.11
  351.1 6.1 %copy-start.10 = (bf16[512,1024]{1,0:T(8,128)(2,1)S(1)}, bf16[512,1024]{1,0:T(8,128)(2,1)}, u32[]{:S(2)}) copy-start(bf16[512,1024]{1,0:T(8,128)(2,1)} %copy-done.9) | copy-start | bytes 3145732
  352.9 10.4 %collective-permute-start.6 = (bf16[64,1024]{1,0:T(8,128)(2,1)S(1)}, bf16[64,1024]{1,0:T(8,128)(2,1)S(1)}, u32[]{:S(2)}, u32[]{:S(2)}) collective-permute-start(bf16[64,1024]{1,0:T(8,128)(2,1)S(1)} %get-tuple-element.27), channel_id=1, source_target_pairs={{16,0},{17,1},{18,2},{19,3},{20,4},{21,5},{22,6},{23,7},{24,8},{25... | collective-permute-start | bytes 393224 | tf_op jit(solution)/shard_map/ppermute | solution.py:42
  354.2 7.8 %collective-permute-start.5 = (bf16[64,1024]{1,0:T(8,128)(2,1)S(1)}, bf16[64,1024]{1,0:T(8,128)(2,1)S(1)}, u32[]{:S(2)}, u32[]{:S(2)}) collective-permute-start(bf16[64,1024]{1,0:T(8,128)(2,1)S(1)} %get-tuple-element.25), channel_id=1, source_target_pairs={{16,0},{17,1},{18,2},{19,3},{20,4},{21,5},{22,6},{23,7},{24,8},{25... | collective-permute-start | bytes 393224 | tf_op jit(solution)/shard_map/ppermute | solution.py:42
  357.2 18.5 %copy-start.4 = (f32[1,5,64,1024]{3,2,1,0:T(8,128)S(1)}, f32[1,5,64,1024]{3,2,1,0:T(8,128)}, u32[]{:S(2)}) copy-start(f32[1,5,64,1024]{3,2,1,0:T(8,128)} %param.13) | copy-start | bytes 3932164
  357.2 20.1 %copy-start.5 = (f32[1024,1024]{1,0:T(8,128)S(1)}, f32[1024,1024]{1,0:T(8,128)}, u32[]{:S(2)}) copy-start(f32[1024,1024]{1,0:T(8,128)} %get-tuple-element.23) | copy-start | bytes 12582916
  362.0 6.8 %collective-permute-start.7 = (bf16[64,1024]{1,0:T(8,128)(2,1)S(1)}, bf16[64,1024]{1,0:T(8,128)(2,1)S(1)}, u32[]{:S(2)}, u32[]{:S(2)}) collective-permute-start(bf16[64,1024]{1,0:T(8,128)(2,1)S(1)} %get-tuple-element.29), channel_id=1, source_target_pairs={{16,0},{17,1},{18,2},{19,3},{20,4},{21,5},{22,6},{23,7},{24,8},{25... | collective-permute-start | bytes 393224 | tf_op jit(solution)/shard_map/ppermute | solution.py:42
  363.3 6.9 %collective-permute-start.8 = (bf16[64,1024]{1,0:T(8,128)(2,1)S(1)}, bf16[64,1024]{1,0:T(8,128)(2,1)S(1)}, u32[]{:S(2)}, u32[]{:S(2)}) collective-permute-start(bf16[64,1024]{1,0:T(8,128)(2,1)S(1)} %get-tuple-element.31), channel_id=1, source_target_pairs={{16,0},{17,1},{18,2},{19,3},{20,4},{21,5},{22,6},{23,7},{24,8},{25... | collective-permute-start | bytes 393224 | tf_op jit(solution)/shard_map/ppermute | solution.py:42
  368.8 6.8 %collective-permute-start.9 = (bf16[64,1024]{1,0:T(8,128)(2,1)S(1)}, bf16[64,1024]{1,0:T(8,128)(2,1)S(1)}, u32[]{:S(2)}, u32[]{:S(2)}) collective-permute-start(bf16[64,1024]{1,0:T(8,128)(2,1)S(1)} %get-tuple-element.33), channel_id=1, source_target_pairs={{16,0},{17,1},{18,2},{19,3},{20,4},{21,5},{22,6},{23,7},{24,8},{25... | collective-permute-start | bytes 393224 | tf_op jit(solution)/shard_map/ppermute | solution.py:42
  375.7 2.7 copy-start.3
Sparse Core Ops, SparseCore 0:
  10.5 45.2 all-gather.10
  58.0 40.1 all-gather.12
  100.4 40.1 all-gather.14
  142.6 40.1 all-gather.16
  185.4 40.1 all-gather.18
  237.6 96.8 all-reduce.1
where the time goes:
time: 391 us
  waiting for transfers between devices  272 us (70%)
  matrix products  52.6 us (13%)
  starting transfers between devices  22.9 us (6%)
  other arithmetic  22 us (6%)
  between operations  14.6 us (4%)
  local copies, waits for them, and re-layouts  6.81 us (2%)
    all_gather x5, waiting for transfers between devices, plain_training(): lax.all_gather(hidden_narrow[i], 'tile', axis=0, tiled=True)  166 us
    psum x1, waiting for transfers between devices, plain_training(): upstream = lax.psum(partial_grad, 'tile')  86 us
    dot_general x5, matrix products, plain_training(): jnp.dot(activation, full_hidden[i], preferred_element_type=jnp.float32)  21.8 us
    ppermute x6, waiting for transfers between devices, to_solver(): return lax.ppermute(value.astype(jnp.bfloat16), 'role', [(1, 0)])  11.5 us
    dot_general x5, matrix products, plain_training(): gradient = jnp.dot(own_inputs.T, slope, preferred_element_type=jnp.float32)  10.8 us
    broadcast_in_dim x3, other arithmetic, body(): return (fields_next[None], out_next[None], hidden_next[None])  10.3 us
    ppermute x3, starting transfers between devices, to_trainer(): return lax.ppermute(value.astype(jnp.bfloat16), 'role', [(0, 1)])  10.2 us
    dot_general x3, matrix products, plain_training(): lax.dot_general(slope, full_hidden[i], (((1,), (1,)), ((), ())), preferre...  8.2 us
  transfers between devices with their start and end apart: 17, of which 11 were waited for; matrix products, arithmetic and copies ran while one was open for 18% of the time, Pallas kernels for 0%

commit v1 on v0

--- a/solution.py
+++ b/solution.py
@@ -63,7 +63,7 @@
     partial_grad = lax.dot_general(
         residual, out_narrow, (((1,), (1,)), ((), ())), preferred_element_type=jnp.float32
     )
-    upstream = lax.psum(partial_grad, "tile")
+    upstream = jnp.sum(lax.all_gather(partial_grad, "tile"), axis=0)
     grad_out = jnp.dot(activation.T, residual, preferred_element_type=jnp.float32)
     sent_out = to_solver(grad_out)
     gradients, sent = ([], [])

time: 391 us -> 467 us (1.19)
  waiting for transfers between devices: 272 us -> 338 us
  other arithmetic: 22 us -> 35.8 us
    psum x1 -> x0, waiting for transfers between devices: 86 us -> none  [plain_training(): upstream = lax.psum(partial_grad, 'tile')]
    all_gather x0 -> x1, waiting for transfers between devices: none -> 85.9 us  [plain_training(): upstream = jnp.sum(lax.all_gather(partial_grad, 'tile'), axis=0)]
    ppermute x3, waiting for transfers between devices: 0.01 us -> 46.9 us  [to_trainer(): return lax.ppermute(value.astype(jnp.bfloat16), 'role', [(0, 1)])]
    all_gather x5, waiting for transfers between devices: 166 us -> 191 us  [plain_training(): lax.all_gather(hidden_narrow[i], 'tile', axis=0, tiled=True)]
    reduce_sum x0 -> x1, other arithmetic: none -> 12.1 us  [plain_training(): upstream = jnp.sum(lax.all_gather(partial_grad, 'tile'), axis=0)]
    ppermute x1, waiting for transfers between devices: 5.41 us -> 0.01 us  [extended(): before = lax.ppermute(last, axis, up)]
  transfers between devices with their start and end apart: 17 -> 17, of which waited for: 11 -> 12; matrix products, arithmetic and copies ran while one was open for 18% -> 15% of each run, Pallas kernels for 0% -> 0%
where the time goes in v1:
time: 467 us; the launch traced here: 466 us
  waiting for transfers between devices  338 us (72%)
  matrix products  49.1 us (11%)
  other arithmetic  35.8 us (8%)
  starting transfers between devices  20.9 us (4%)
  between operations  14.5 us (3%)
  local copies, waits for them, and re-layouts  7.28 us (2%)
    all_gather x5, waiting for transfers between devices, plain_training(): lax.all_gather(hidden_narrow[i], 'tile', axis=0, tiled=True)  191 us
    all_gather x1, waiting for transfers between devices, plain_training(): upstream = jnp.sum(lax.all_gather(partial_grad, 'tile'), axis=0)  85.9 us
    ppermute x3, waiting for transfers between devices, to_trainer(): return lax.ppermute(value.astype(jnp.bfloat16), 'role', [(0, 1)])  46.9 us
    dot_general x5, matrix products, plain_training(): jnp.dot(activation, full_hidden[i], preferred_element_type=jnp.float32)  21 us
    reduce_sum x1, other arithmetic, plain_training(): upstream = jnp.sum(lax.all_gather(partial_grad, 'tile'), axis=0)  12.1 us
    broadcast_in_dim x3, other arithmetic, body(): return (fields_next[None], out_next[None], hidden_next[None])  11.6 us
    dot_general x5, matrix products, plain_training(): gradient = jnp.dot(own_inputs.T, slope, preferred_element_type=jnp.float32)  10.2 us
  transfers between devices with their start and end apart: 17, of which 12 were waited for; matrix products, arithmetic and copies ran while one was open for 15% of the time, Pallas kernels for 0%

profile of v1, /device:TPU:0, one launch (start us, length us, event | category | flops | bytes accessed | tf_op | source)
XLA Modules:
  0.0 465.9 jit_solution(2993543887786085255)
XLA Ops:
  7.2 0.0 all-gather.13.cloned.1.call-start
  7.2 2.4 bitcast_convert_fusion.1
  9.6 2.0 fusion.60
  11.6 0.0 all-gather.15.cloned.1.call-start
  11.7 0.7 all-gather.15.cloned.1.call-update
  12.4 0.7 all-gather.17.cloned.1.call-update
  13.1 0.5 all-gather.19.cloned.1.call-update
  13.7 0.5 all-gather.21.cloned.1.call-update
  14.3 0.0 all-gather.23.cloned.1.call-start
  14.3 3.8 bitcast_convert_fusion
  18.1 37.8 %all-gather.13.cloned.1.call-done = bf16[1,1024,1024]{2,1,0:T(8,128)(2,1)} async-done(((bf16[1,64,1024]{2,1,0:T(8,128)(2,1)}), bf16[1,1024,1024]{2,1,0:T(8,128)(2,1)}) %all-gather.13.cloned.1.call-update) | async-done | bytes 2097168 | tf_op jit(solution)/shard_map/all_gather | solution.py:52
  55.9 4.3 multiply_convert_fusion.10
  60.3 38.0 %all-gather.15.cloned.1.call-done = bf16[1,1024,1024]{2,1,0:T(8,128)(2,1)} async-done(((bf16[1,64,1024]{2,1,0:T(8,128)(2,1)}), bf16[1,1024,1024]{2,1,0:T(8,128)(2,1)}) %all-gather.15.cloned.1.call-update) | async-done | bytes 2097168 | tf_op jit(solution)/shard_map/all_gather | solution.py:52
  98.3 4.4 multiply_convert_fusion.9
  102.7 38.6 %all-gather.17.cloned.1.call-done = bf16[1,1024,1024]{2,1,0:T(8,128)(2,1)} async-done(((bf16[1,64,1024]{2,1,0:T(8,128)(2,1)}), bf16[1,1024,1024]{2,1,0:T(8,128)(2,1)}) %all-gather.17.cloned.1.call-update) | async-done | bytes 2097168 | tf_op jit(solution)/shard_map/all_gather | solution.py:52
  141.3 4.3 multiply_convert_fusion.8
  145.6 38.5 %all-gather.19.cloned.1.call-done = bf16[1,1024,1024]{2,1,0:T(8,128)(2,1)} async-done(((bf16[1,64,1024]{2,1,0:T(8,128)(2,1)}), bf16[1,1024,1024]{2,1,0:T(8,128)(2,1)}) %all-gather.19.cloned.1.call-update) | async-done | bytes 2097168 | tf_op jit(solution)/shard_map/all_gather | solution.py:52
  184.1 4.7 %multiply_convert_fusion.7 = (bf16[512,1024]{1,0:T(8,128)(2,1)}, f32[512,1024]{1,0:T(8,128)}) fusion(bf16[512,1024]{1,0:T(8,128)(2,1)S(1)} %get-tuple-element.18, bf16[1,1024,1024]{2,1,0:T(8,128)(2,1)} %all-gather.19.cloned.1.call-done), kind=kOutput, calls=%fused_computation.45 | convolution fusion | flops 1076363264 | bytes 6291456 | tf_op jit(solution)/shard_map/dot_general | solution.py:58
  188.7 38.1 %all-gather.21.cloned.1.call-done = bf16[1,1024,1024]{2,1,0:T(8,128)(2,1)} async-done(((bf16[1,64,1024]{2,1,0:T(8,128)(2,1)}), bf16[1,1024,1024]{2,1,0:T(8,128)(2,1)}) %all-gather.21.cloned.1.call-update) | async-done | bytes 2097168 | tf_op jit(solution)/shard_map/all_gather | solution.py:52
  226.8 3.3 fusion.10
  230.2 3.7 multiply_convert_fusion.5
  233.9 1.0 copy-done.19
  234.8 4.2 fusion.64
  239.1 0.7 copy-done.10
  239.7 0.1 pad_maximum_fusion.5
  239.9 0.3 collective-permute-start
  240.2 4.9 %collective-permute-start.4 = (bf16[1024,1024]{1,0:T(8,128)(2,1)}, bf16[1024,1024]{1,0:T(8,128)(2,1)}, u32[]{:S(2)}, u32[]{:S(2)}) collective-permute-start(bf16[1024,1024]{1,0:T(8,128)(2,1)} %bitcast_convert_fusion), channel_id=1, source_target_pairs={{0,16},{1,17},{2,18},{3,19},{4,20},{5,21},{6,22},{7,23},{8,24},{9,... | collective-permute-start | bytes 6291464 | tf_op jit(solution)/shard_map/ppermute | solution.py:38
  245.1 3.8 collective-permute-start.1
  248.8 0.1 maximum_reduce_fusion
  249.0 4.1 fusion.61
  253.1 1.5 collective-permute-start.3
  254.5 4.1 collective-permute-done.1
  258.6 0.7 fusion.6
  259.3 2.4 fusion.59
  261.7 1.7 collective-permute-start.2
  263.4 2.1 collective-permute-start.10
  265.6 46.9 %collective-permute-done.2 = bf16[512,1024]{1,0:T(8,128)(2,1)S(1)} collective-permute-done((bf16[512,1024]{1,0:T(8,128)(2,1)}, bf16[512,1024]{1,0:T(8,128)(2,1)S(1)}, u32[]{:S(2)}, u32[]{:S(2)}) %collective-permute-start.2) | collective-permute-done | bytes 1048608 | tf_op jit(solution)/shard_map/ppermute | solution.py:38
  312.5 2.0 gather_fusion
  314.5 3.4 select_bitcast_fusion
  317.9 6.7 %fusion.1 = f32[1,1024,1024]{2,1,0:T(8,128)} fusion(f32[1024,1024]{1,0:T(8,128)} %get-tuple-element.23, f32[1,1024,1024]{2,1,0:T(8,128)S(1)} %copy-done.2, bf16[1024,1024]{1,0:T(8,128)(2,1)} %collective-permute-done.3, bf16[1024,1024]{1,0:T(8,128)(2,1)} %collective-permute-done.4, pred[]{:T(512)S(6)} %eq.4), kind=kLoop, calls=%fused_computation.4 | loop fusion | flops 9437184 | bytes 16777216 | tf_op jit(solution)/shard_map/broadcast_in_dim | solution.py:117
  324.6 85.9 %all-gather.23.cloned.1.call-done = f32[8192,1024]{1,0:T(8,128)} async-done(((f32[512,1024]{1,0:T(8,128)}), f32[8192,1024]{1,0:T(8,128)}) %all-gather.23.cloned.1.call-update) | async-done | bytes 33554448 | tf_op jit(solution)/shard_map/all_gather | solution.py:66
  410.5 12.1 %reduce_sum.9 = f32[512,1024]{1,0:T(8,128)S(1)} reduce(f32[16,512,1024]{2,1,0:T(8,128)} %bitcast.104, f32[]{:T(128)} %constant.19.clone.1), dimensions={0}, to_apply=%region_0.1 | reduce | flops 7864320 | bytes 35651588 | tf_op jit(solution)/shard_map/reduce_sum | solution.py:66
  422.6 2.5 multiply_convert_fusion.4
  425.1 0.3 copy-done.23
  425.4 1.6 multiply_convert_fusion.3
  427.1 0.6 copy-done.22
  427.7 1.6 multiply_convert_fusion.2
  429.3 0.6 copy-done.21
  429.9 2.6 multiply_convert_fusion.1
  432.5 4.3 bitcast_dynamic-update-slice_fusion.4
  436.8 1.8 bitcast_dynamic-update-slice_fusion.3
  438.7 1.3 collective-permute-start.6
  440.0 1.3 collective-permute-start.5
  441.3 1.3 bitcast_dynamic-update-slice_fusion.2
  442.6 1.3 collective-permute-start.7
  443.9 1.4 bitcast_dynamic-update-slice_fusion.1
  445.3 1.3 collective-permute-start.8
  446.7 1.3 bitcast_dynamic-update-slice_fusion
  448.0 1.8 collective-permute-done.5
  449.8 1.3 collective-permute-start.9
  451.1 1.5 collective-permute-done.7
  452.6 2.8 collective-permute-done.8
  455.4 2.1 collective-permute-done.9
  457.5 1.6 fusion.35
  (61 shorter events, 0.3 us)
Async XLA Ops:
  7.2 48.8 %copy-start = (bf16[512,1024]{1,0:T(8,128)(2,1)S(1)}, bf16[512,1024]{1,0:T(8,128)(2,1)}, u32[]{:S(2)}) copy-start(bf16[512,1024]{1,0:T(8,128)(2,1)} %param.10) | copy-start | bytes 3145732
  7.2 48.8 %all-gather.13.cloned.1.call-start = ((), (), s32[]{:S(2)}) async-start(), calls=%async_computation | async-start | bytes 2228224 | tf_op jit(solution)/shard_map/all_gather | solution.py:52
  11.6 86.7 %all-gather.15.cloned.1.call-start = ((), (), s32[]{:S(2)}) async-start(), calls=%async_computation.1 | async-start | bytes 2228224 | tf_op jit(solution)/shard_map/all_gather | solution.py:52
  12.4 128.9 %all-gather.17.cloned.1.call-start = ((), (), s32[]{:S(2)}) async-start(), calls=%async_computation.2 | async-start | bytes 2228224 | tf_op jit(solution)/shard_map/all_gather | solution.py:52
  13.1 171.0 %all-gather.19.cloned.1.call-start = ((), (), s32[]{:S(2)}) async-start(), calls=%async_computation.3 | async-start | bytes 2228224 | tf_op jit(solution)/shard_map/all_gather | solution.py:52
  13.7 213.2 %all-gather.21.cloned.1.call-start = ((), (), s32[]{:S(2)}) async-start(), calls=%async_computation.4 | async-start | bytes 2228224 | tf_op jit(solution)/shard_map/all_gather | solution.py:52
  14.3 396.2 %all-gather.23.cloned.1.call-start = ((), (), s32[]{:S(2)}) async-start(), calls=%async_computation.5 | async-start | bytes 35651584 | tf_op jit(solution)/shard_map/all_gather | solution.py:66
  60.3 42.4 %copy-start.13 = (bf16[512,1024]{1,0:T(8,128)(2,1)}, bf16[512,1024]{1,0:T(8,128)(2,1)S(1)}, u32[]{:S(2)}) copy-start(bf16[512,1024]{1,0:T(8,128)(2,1)S(1)} %get-tuple-element.14) | copy-start | bytes 3145732
  102.7 42.9 %copy-start.12 = (bf16[512,1024]{1,0:T(8,128)(2,1)}, bf16[512,1024]{1,0:T(8,128)(2,1)S(1)}, u32[]{:S(2)}) copy-start(bf16[512,1024]{1,0:T(8,128)(2,1)S(1)} %get-tuple-element.16) | copy-start | bytes 3145732
  145.6 43.2 %copy-start.11 = (bf16[512,1024]{1,0:T(8,128)(2,1)}, bf16[512,1024]{1,0:T(8,128)(2,1)S(1)}, u32[]{:S(2)}) copy-start(bf16[512,1024]{1,0:T(8,128)(2,1)S(1)} %get-tuple-element.18) | copy-start | bytes 3145732
  226.8 3.3 copy-start.1
  230.2 3.7 copy-start.6
  233.8 1.0 copy-start.19
  239.0 0.7 copy-start.10
  239.7 9.2 %copy-start.7 = (f32[512,1024]{1,0:T(8,128)S(1)}, f32[512,1024]{1,0:T(8,128)}, u32[]{:S(2)}) copy-start(f32[512,1024]{1,0:T(8,128)} %copy-done.6) | copy-start | bytes 6291460
  239.7 9.2 %copy-start.20 = (bf16[512,1024]{1,0:T(8,128)(2,1)S(1)}, bf16[512,1024]{1,0:T(8,128)(2,1)}, u32[]{:S(2)}) copy-start(bf16[512,1024]{1,0:T(8,128)(2,1)} %copy-done.19) | copy-start | bytes 3145732
  239.9 9.0 %collective-permute-start = (f32[513,1]{1,0:T(8,128)S(1)}, f32[513,1]{1,0:T(8,128)S(1)}, u32[]{:S(2)}, u32[]{:S(2)}) collective-permute-start(f32[513,1]{1,0:T(8,128)S(1)} %get-tuple-element.7), channel_id=1, source_target_pairs={{0,1},{1,2},{2,3},{3,4},{4,5},{5,6},{6,7},{7,8},{8,9},{9,10},{10,1... | collective-permute-start | bytes 6164 | tf_op jit(solution)/shard_map/ppermute | solution.py:16
  240.2 77.8 %collective-permute-start.4 = (bf16[1024,1024]{1,0:T(8,128)(2,1)}, bf16[1024,1024]{1,0:T(8,128)(2,1)}, u32[]{:S(2)}, u32[]{:S(2)}) collective-permute-start(bf16[1024,1024]{1,0:T(8,128)(2,1)} %bitcast_convert_fusion), channel_id=1, source_target_pairs={{0,16},{1,17},{2,18},{3,19},{4,20},{5,21},{6,22},{7,23},{8,24},{9,... | collective-permute-start | bytes 6291464 | tf_op jit(solution)/shard_map/ppermute | solution.py:38
  245.1 13.5 %collective-permute-start.1 = (f32[513,1]{1,0:T(8,128)S(1)}, f32[513,1]{1,0:T(8,128)S(1)}, u32[]{:S(2)}, u32[]{:S(2)}) collective-permute-start(f32[513,1]{1,0:T(8,128)S(1)} %get-tuple-element.8), channel_id=1, source_target_pairs={{1,0},{2,1},{3,2},{4,3},{5,4},{6,5},{7,6},{8,7},{9,8},{10,9},{11,1... | collective-permute-start | bytes 6164 | tf_op jit(solution)/shard_map/ppermute | solution.py:17
  253.1 64.9 %collective-permute-start.3 = (bf16[1024,1024]{1,0:T(8,128)(2,1)}, bf16[1024,1024]{1,0:T(8,128)(2,1)}, u32[]{:S(2)}, u32[]{:S(2)}) collective-permute-start(bf16[1024,1024]{1,0:T(8,128)(2,1)} %get-tuple-element.22), channel_id=1, source_target_pairs={{16,0},{17,1},{18,2},{19,3},{20,4},{21,5},{22,6},{23,7},{24,8},{25... | collective-permute-start | bytes 6291464 | tf_op jit(solution)/shard_map/ppermute | solution.py:42
  258.6 0.7 copy-start.15
  259.3 6.3 %copy-start.14 = (s32[512]{0:T(512)S(1)}, s32[512]{0:T(512)}, u32[]{:S(2)}) copy-start(s32[512]{0:T(512)} %param.11) | copy-start | bytes 6148
  261.7 50.7 %collective-permute-start.2 = (bf16[512,1024]{1,0:T(8,128)(2,1)}, bf16[512,1024]{1,0:T(8,128)(2,1)S(1)}, u32[]{:S(2)}, u32[]{:S(2)}) collective-permute-start(bf16[512,1024]{1,0:T(8,128)(2,1)} %get-tuple-element.5), channel_id=1, source_target_pairs={{0,16},{1,17},{2,18},{3,19},{4,20},{5,21},{6,22},{7,23},{8,24},{9,... | collective-permute-start | bytes 3145736 | tf_op jit(solution)/shard_map/ppermute | solution.py:38
  263.4 194.0 %collective-permute-start.10 = (bf16[5,64,1024]{2,1,0:T(8,128)(2,1)}, bf16[5,64,1024]{2,1,0:T(8,128)(2,1)}, u32[]{:S(2)}, u32[]{:S(2)}) collective-permute-start(bf16[5,64,1024]{2,1,0:T(8,128)(2,1)} %bitcast_convert_fusion.1), channel_id=1, source_target_pairs={{0,16},{1,17},{2,18},{3,19},{4,20},{5,21},{6,22},{7,23},{8,24},{9,... | collective-permute-start | bytes 1966088 | tf_op jit(solution)/shard_map/ppermute | solution.py:38
  314.5 3.4 copy-start.2
  422.6 2.5 copy-start.18
  422.6 2.8 copy-start.23
  425.1 2.0 copy-start.4
  425.4 1.7 copy-start.17
  425.4 2.2 copy-start.22
  427.7 1.7 copy-start.16
  427.7 2.2 copy-start.21
  429.3 3.2 copy-start.8
  436.8 4.5 copy-start.9
  436.8 9.8 %copy-start.5 = (bf16[512,1024]{1,0:T(8,128)(2,1)S(1)}, bf16[512,1024]{1,0:T(8,128)(2,1)}, u32[]{:S(2)}) copy-start(bf16[512,1024]{1,0:T(8,128)(2,1)} %copy-done.4) | copy-start | bytes 3145732
  438.7 12.4 %collective-permute-start.6 = (bf16[64,1024]{1,0:T(8,128)(2,1)S(1)}, bf16[64,1024]{1,0:T(8,128)(2,1)S(1)}, u32[]{:S(2)}, u32[]{:S(2)}) collective-permute-start(bf16[64,1024]{1,0:T(8,128)(2,1)S(1)} %get-tuple-element.27), channel_id=1, source_target_pairs={{16,0},{17,1},{18,2},{19,3},{20,4},{21,5},{22,6},{23,7},{24,8},{25... | collective-permute-start | bytes 393224 | tf_op jit(solution)/shard_map/ppermute | solution.py:42
  440.0 9.8 %collective-permute-start.5 = (bf16[64,1024]{1,0:T(8,128)(2,1)S(1)}, bf16[64,1024]{1,0:T(8,128)(2,1)S(1)}, u32[]{:S(2)}, u32[]{:S(2)}) collective-permute-start(bf16[64,1024]{1,0:T(8,128)(2,1)S(1)} %get-tuple-element.25), channel_id=1, source_target_pairs={{16,0},{17,1},{18,2},{19,3},{20,4},{21,5},{22,6},{23,7},{24,8},{25... | collective-permute-start | bytes 393224 | tf_op jit(solution)/shard_map/ppermute | solution.py:42
  442.6 10.0 %collective-permute-start.7 = (bf16[64,1024]{1,0:T(8,128)(2,1)S(1)}, bf16[64,1024]{1,0:T(8,128)(2,1)S(1)}, u32[]{:S(2)}, u32[]{:S(2)}) collective-permute-start(bf16[64,1024]{1,0:T(8,128)(2,1)S(1)} %get-tuple-element.29), channel_id=1, source_target_pairs={{16,0},{17,1},{18,2},{19,3},{20,4},{21,5},{22,6},{23,7},{24,8},{25... | collective-permute-start | bytes 393224 | tf_op jit(solution)/shard_map/ppermute | solution.py:42
  443.9 13.6 %copy-start.3 = (f32[1,5,64,1024]{3,2,1,0:T(8,128)S(1)}, f32[1,5,64,1024]{3,2,1,0:T(8,128)}, u32[]{:S(2)}) copy-start(f32[1,5,64,1024]{3,2,1,0:T(8,128)} %param.13) | copy-start | bytes 3932164
  445.3 10.0 %collective-permute-start.8 = (bf16[64,1024]{1,0:T(8,128)(2,1)S(1)}, bf16[64,1024]{1,0:T(8,128)(2,1)S(1)}, u32[]{:S(2)}, u32[]{:S(2)}) collective-permute-start(bf16[64,1024]{1,0:T(8,128)(2,1)S(1)} %get-tuple-element.31), channel_id=1, source_target_pairs={{16,0},{17,1},{18,2},{19,3},{20,4},{21,5},{22,6},{23,7},{24,8},{25... | collective-permute-start | bytes 393224 | tf_op jit(solution)/shard_map/ppermute | solution.py:42
  449.8 7.7 %collective-permute-start.9 = (bf16[64,1024]{1,0:T(8,128)(2,1)S(1)}, bf16[64,1024]{1,0:T(8,128)(2,1)S(1)}, u32[]{:S(2)}, u32[]{:S(2)}) collective-permute-start(bf16[64,1024]{1,0:T(8,128)(2,1)S(1)} %get-tuple-element.33), channel_id=1, source_target_pairs={{16,0},{17,1},{18,2},{19,3},{20,4},{21,5},{22,6},{23,7},{24,8},{25... | collective-permute-start | bytes 393224 | tf_op jit(solution)/shard_map/ppermute | solution.py:42
Sparse Core Ops, SparseCore 0:
  11.7 44.1 all-gather.12
  58.1 40.1 all-gather.14
  101.0 40.1 all-gather.16
  143.8 40.1 all-gather.18
  186.6 40.1 all-gather.20
  239.2 171.2 all-gather.22
